TPU v7x, 512 devices: a whole 4x8x8 slice. The times are simulated.
512 devices in a mesh: stream: 8 (over y), span: 16 (over z, core), vert: 4 (over x).
Axes of the slice: x: 4, y: 8, z: 8, core: 2. Of those that a mesh axis runs over, the one named last changes fastest.
Arguments:
- fields: float32 [5, 128, 256, 1024], P(None, 'vert', 'span', 'stream'), may hold values from -6 to 6
- solid_frac: float32 [128, 256, 1024], P('vert', 'span', 'stream'), may hold values from 0 to 1
- panels: float32 [32768, 5, 256], P(('stream', 'span', 'vert')), may hold values from -0.015625 to 0.015625
- panel_owner: int32 [32768, 1], P(('stream', 'span', 'vert')), may hold values from 0 to 63; in each aligned block of 64 rows (0 to 63, 64 to 127, ...) at most 2 rows name the same one
- deck_cells: int32 [4, 16, 8, 2048], P('vert', 'span', 'stream'), may hold values from 0 to 65535
- deck_geom: float32 [4, 16, 8, 3, 2048], P('vert', None, 'stream'), may hold values from -6 to 6
- strip_ids: int32 [4, 16, 8, 2048], P('vert', None, 'stream'), may hold values from 0 to 63, as said below
- mode_shapes: float32 [3, 64, 32], replicated, may hold values from -0.0034179688 to 0.0034179688
Outputs:
- new_fields: float32 [5, 128, 256, 1024], P(None, 'vert', 'span', 'stream')
- modal_force: float32 [32], replicated
Inputs may be any that keep to these rules, and one draw needn't show every extreme that they name: `panel_owner`: tile number s * 4 + v for along-deck tile s and vertical tile v. Among the 64 panels of one device no tile is named more than 2 times; some device names some tile exactly 2 times. `strip_ids`: cells of along-deck tile s belong to strips s * 4 to (s + 1) * 4 - 1.
All inputs are finite; a program needn't handle non-finite values.
Results may differ from a plain program's by a relative error of at most 0.00012.
Values sent between devices are 32-bit elements; how exact they have to be, the bound alone decides.
No kernel may reach another device: no remote copies, remote signals or barrier semaphores. Data moves between devices by JAX's collectives and lax.ppermute only.
A program may use at most 128 MiB of HBM per device.

v0:
```python
import math
import jax
import jax.numpy as jnp
from jax import lax
from jax.sharding import PartitionSpec as P

CAP = 2
time_step = 0.15
viscous = 0.05
heat_diff = 0.03
sound_sq = 1.0
buoyant = 0.5
penalty = 0.5
relax_time = 0.5
relax_depth = 8.0
wave_cols = 16


def extended(block, sides, width):
    for axis, dim in sides:
        count = lax.axis_size(axis)
        forward = [(i, i + 1) for i in range(count - 1)]
        backward = [(target, source) for source, target in forward]
        low = lax.ppermute(
            lax.slice_in_dim(block, block.shape[dim] - width, None, axis=dim), axis, forward
        )
        high = lax.ppermute(lax.slice_in_dim(block, 0, width, axis=dim), axis, backward)
        block = jnp.concatenate([low, block, high], axis=dim)
    return block


def wave_basis(heights, widths, total_z, total_y, spec):
    modes = jnp.arange(spec, dtype=jnp.int32)
    across = (modes % wave_cols)[:, None, None]
    upward = (modes // wave_cols)[:, None, None]
    period = total_y * total_z
    phase = (
        across * widths[None, None, :] * total_z + upward * heights[None, :, None] * total_y
    ) % period
    angle = phase.astype(jnp.float32) * (2.0 * math.pi / period)
    return jnp.concatenate([jnp.cos(angle), jnp.sin(angle)], axis=0)


def relax_weights(positions, limit):
    spots = positions.astype(jnp.float32)
    return jnp.where(positions < limit, jnp.exp(-spots / relax_depth) / relax_time, 0.0)


def rates(padded, solid_frac, relax_rate, target_plane):
    centre = padded[:, 1:-1, 1:-1, 1:-1]
    east_side = padded[:, 1:-1, 1:-1, 2:]
    west_side = padded[:, 1:-1, 1:-1, :-2]
    north_side = padded[:, 1:-1, 2:, 1:-1]
    south_side = padded[:, 1:-1, :-2, 1:-1]
    upper_side = padded[:, 2:, 1:-1, 1:-1]
    lower_side = padded[:, :-2, 1:-1, 1:-1]
    grad_x = 0.5 * (east_side - west_side)
    grad_y = 0.5 * (north_side - south_side)
    grad_z = 0.5 * (upper_side - lower_side)
    laplace = (
        east_side + west_side + north_side + south_side + upper_side + lower_side - 6.0 * centre
    )
    speed_x = centre[0]
    speed_y = centre[1]
    speed_z = centre[2]
    carried = speed_x * grad_x + speed_y * grad_y + speed_z * grad_z
    coeffs = jnp.array([viscous, viscous, viscous, viscous, heat_diff], jnp.float32)[
        :, None, None, None
    ]
    damping = solid_frac / penalty
    nudging = relax_rate[None, None, None, :] * (target_plane[:, :, :, None] - centre)
    common = coeffs * laplace - carried + nudging
    extra_terms = jnp.stack(
        [
            -grad_x[3] - damping * speed_x,
            -grad_y[3] - damping * speed_y,
            -grad_z[3] - damping * speed_z + buoyant * centre[4],
            -sound_sq * (grad_x[0] + grad_y[1] + grad_z[2]),
            jnp.zeros_like(speed_x),
        ]
    )
    return common + extra_terms


def pack_slots(flat_panels, target_tile, chosen, tile_count):
    running = jnp.cumsum(chosen, axis=0) - 1
    slot_rank = jnp.sum(chosen * running, axis=1)
    slot_index = target_tile * CAP + slot_rank
    dispatch = (
        slot_index[None, :] == jnp.arange(tile_count * CAP, dtype=jnp.int32)[:, None]
    ).astype(jnp.float32)
    return jnp.dot(dispatch, flat_panels, precision=lax.Precision.HIGHEST)


def strip_forces(traction, labels, strip_count):
    columns = jnp.arange(strip_count, dtype=jnp.int32)

    def add_row(running, item_pair):
        row_values, row_labels = item_pair
        member = (row_labels[:, None] == columns[None, :]).astype(jnp.float32)
        return (running + jnp.dot(row_values, member, precision=lax.Precision.HIGHEST), None)

    start_value = jnp.zeros((traction.shape[1], strip_count), jnp.float32)
    summed, ignored = lax.scan(add_row, start_value, (traction, labels))
    return summed


def on_device(
    fields, solid_frac, panels, panel_owner, deck_cells, deck_geom, strip_ids, mode_shapes
):
    depth_cells = fields.shape[1]
    span_cells = fields.shape[2]
    wind_cells = fields.shape[3]
    n_span = lax.axis_size("span")
    n_vert = lax.axis_size("vert")
    stream_pos = lax.axis_index("stream")
    span_pos = lax.axis_index("span")
    vert_pos = lax.axis_index("vert")
    tile_count = n_span * n_vert
    held_panels = panels.shape[0]
    spec_cols = panels.shape[2]
    flat_panels = panels.reshape(held_panels, 5 * spec_cols)
    target_tile = panel_owner[:, 0]
    chosen = (target_tile[:, None] == jnp.arange(tile_count, dtype=jnp.int32)[None, :]).astype(
        jnp.int32
    )
    outgoing = pack_slots(flat_panels, target_tile, chosen, tile_count)
    arrived = lax.all_to_all(
        outgoing.reshape(tile_count, CAP * 5 * spec_cols),
        ("span", "vert"),
        split_axis=0,
        concat_axis=0,
        tiled=True,
    )
    coeffs = jnp.sum(arrived.reshape(-1, 5 * spec_cols), axis=0)
    coeffs = coeffs.reshape(5, spec_cols)
    heights = vert_pos * depth_cells + jnp.arange(depth_cells, dtype=jnp.int32)
    widths = span_pos * span_cells + jnp.arange(span_cells, dtype=jnp.int32)
    wave_table = wave_basis(
        heights, widths, depth_cells * n_vert, span_cells * n_span, spec_cols // 2
    )
    wave_table = wave_table.reshape(spec_cols, depth_cells * span_cells)
    partial_value = jnp.dot(coeffs, wave_table, precision=lax.Precision.HIGHEST)
    inflow_plane = lax.psum(partial_value, "stream").reshape(5, depth_cells, span_cells)
    target_plane = inflow_plane + jnp.array([1.0, 0.0, 0.0, 0.0, 0.0], jnp.float32)[:, None, None]
    wind_first = stream_pos * wind_cells
    relax_rate = relax_weights(
        wind_first + jnp.arange(wind_cells, dtype=jnp.int32), wind_cells // 2
    )

    def advance(state):
        padded = extended(state, (("stream", 3), ("span", 2), ("vert", 1)), 1)
        return rates(padded, solid_frac, relax_rate, target_plane)

    first_update = fields + time_step * advance(fields)
    second_rate = advance(first_update)
    new_fields = 0.5 * (fields + first_update + time_step * second_rate)
    pressure = new_fields[3].reshape(-1)
    sampled = pressure[deck_cells[0, 0, 0]]
    strip_count = mode_shapes.shape[1]
    rows_all = lax.all_gather(sampled.reshape(1, 1, 1, -1), "span", axis=1, tiled=True)
    traction = rows_all[0, :, 0][:, None, :] * deck_geom[0, :, 0]
    forces = strip_forces(traction, strip_ids[0, :, 0], strip_count)
    modal_part = jnp.einsum("cj,cjm->m", forces, mode_shapes, precision=lax.Precision.HIGHEST)
    modal_force = lax.psum(modal_part, ("stream", "vert"))
    return (new_fields, modal_force)


def solution(mesh):
    return jax.shard_map(
        on_device,
        mesh=mesh,
        in_specs=(
            P(None, "vert", "span", "stream"),
            P("vert", "span", "stream"),
            P(("stream", "span", "vert"), None, None),
            P(("stream", "span", "vert"), None),
            P("vert", "span", "stream", None),
            P("vert", None, "stream", None, None),
            P("vert", None, "stream", None),
            P(),
        ),
        out_specs=(P(None, "vert", "span", "stream"), P()),
        check_vma=False,
    )
```

profile of v0, /device:TPU:64, one launch (start us, length us, event | category | flops | bytes accessed | tf_op | source)
XLA Modules:
  0.0 263.3 jit_solution(5278629360200519969)
XLA Ops:
  0.6 2.2 fusion.52
  5.3 4.5 %collective-permute-start.1 = (f32[5,32,16,1]{1,2,3,0:T(8,128)S(1)}, f32[5,32,16,1]{1,2,3,0:T(8,128)S(1)}, u32[]{:S(2)}, u32[]{:S(2)}) collective-permute-start(f32[5,32,16,1]{1,2,3,0:T(8,128)S(1)} %copy.56), channel_id=1, source_target_pairs={{0,64},{64,128},{128,192},{192,256},{256,320},{320,384},{384,448},... | collective-permute-start | bytes 30728 | tf_op jit(solution)/shard_map/ppermute | solution.py:24
  12.2 13.3 %all-to-all-start = ((f32[64,1,2560]{2,1,0:T(1,128)}), f32[64,1,2560]{2,1,0:T(1,128)}, u32[]{:S(2)}, u32[]{:S(2)}) async-start(f32[64,1,2560]{2,1,0:T(1,128)} %all_to_all.8), calls=%async_computation | async-start | bytes 1310720 | tf_op jit(solution)/shard_map/all_to_all | solution.py:128
  30.7 2.5 pad_maximum_fusion.39
  33.2 2.0 collective-permute-start.2
  35.2 2.3 collective-permute-start.3
  37.5 4.0 %collective-permute-done.2 = f32[5,32,1,130]{3,2,1,0:T(1,128)S(1)} collective-permute-done((f32[5,32,1,130]{3,2,1,0:T(1,128)S(1)}, f32[5,32,1,130]{3,2,1,0:T(1,128)S(1)}, u32[]{:S(2)}, u32[]{:S(2)}) %collective-permute-start.2) | collective-permute-done | bytes 83232 | tf_op jit(solution)/shard_map/ppermute | solution.py:27
  44.5 4.7 %collective-permute-start.5 = (f32[5,1,18,130]{3,2,1,0:T(8,128)S(1)}, f32[5,1,18,130]{3,2,1,0:T(8,128)S(1)}, u32[]{:S(2)}, u32[]{:S(2)}) collective-permute-start(f32[5,1,18,130]{3,2,1,0:T(8,128)S(1)} %get-tuple-element.71), channel_id=1, source_target_pairs={{0,1},{1,2},{2,3},{4,5},{5,6},{6,7},{8,9},{9,10},{10,11},{12,13},{... | collective-permute-start | bytes 140408 | tf_op jit(solution)/shard_map/ppermute | solution.py:24
  51.7 3.2 %broadcast_multiply_fusion.3 = (f32[5,32,16,128]{3,2,1,0:T(8,128)S(1)}, f32[5,32,16,128]{3,2,1,0:T(8,128)S(1)}) fusion(f32[5,1,18,130]{3,2,1,0:T(8,128)S(1)} %collective-permute-done.4, f32[5,32,1,130]{3,2,1,0:T(1,128)S(1)} %collective-permute-done.2, f32[5,32,16,1]{3,2,1,0:T(8,128)S(1)} %copy.37, f32[5,32,16,128]{3,2,1,0:T(8,128)S(1)} %copy-done.1, ...), kind=kLoop, calls=%fused_computation.50 | loop fusion | flops 5242880 | bytes 4212640 | tf_op jit(solution)/shard_map/mul | solution.py:59
  58.7 2.6 %reduce = f32[64,2560]{1,0:T(8,128)S(1)} reduce(f32[64,1,2560]{2,1,0:T(1,128)} %all-to-all-done, f32[]{:T(128)} %constant.123), dimensions={1}, to_apply=%all_to_all.7.reduce_sub_computation | reduce | bytes 1310724 | tf_op jit(solution)/shard_map/all_to_all | solution.py:128
  63.1 30.8 %psum.14 = f32[5,32,16]{2,1,0:T(8,128)S(1)} all-reduce(f32[5,32,16]{2,1,0:T(8,128)S(1)} %reshape.200), channel_id=1, replica_groups=mesh['stream'=8,'span'=16,'vert'=4] {'stream'}, use_global_device_ids=true, to_apply=%region_3.4 | all-reduce | flops 2560 | bytes 20480 | tf_op jit(solution)/shard_map/psum | solution.py:144
  94.0 7.5 %multiply_add_fusion = f32[5,32,16,128]{3,2,1,0:T(8,128)S(1)} fusion(f32[5,32,16,128]{3,2,1,0:T(8,128)S(1)} %copy-done.1, f32[5,32,16,128]{3,2,1,0:T(8,128)} %broadcast_dynamic-update-slice_fusion.1, f32[5,32,16]{2,1,0:T(8,128)S(1)} %broadcast_add_fusion.1, f32[128]{0:T(128)S(1)} %compare_select_fusion.1, f32[32,16,128]{2,1,0:T(8,128)} %get-tuple-element.87, ...), kind=kLoop, calls=%fused_computation.45 | loop fusion | flops 13434880 | bytes 5009844 | tf_op jit(solution)/shard_map/add | solution.py:155
  108.5 4.5 %collective-permute-start.7 = (f32[5,32,16,1]{1,2,3,0:T(8,128)S(1)}, f32[5,32,16,1]{1,2,3,0:T(8,128)S(1)}, u32[]{:S(2)}, u32[]{:S(2)}) collective-permute-start(f32[5,32,16,1]{1,2,3,0:T(8,128)S(1)} %copy.46), channel_id=1, source_target_pairs={{0,64},{64,128},{128,192},{192,256},{256,320},{320,384},{384,448},... | collective-permute-start | bytes 30728 | tf_op jit(solution)/shard_map/ppermute | solution.py:24
  116.4 2.9 %pad_maximum_fusion.36 = (f32[5,32,1,130]{3,2,1,0:T(1,128)S(1)}, f32[5,32,1,130]{3,2,1,0:T(1,128)S(1)}) fusion(f32[5,32,16,1]{3,2,1,0:T(8,128)} %copy.45, f32[5,32,16,128]{3,2,1,0:T(8,128)S(1)} %multiply_add_fusion, f32[5,32,16,1]{3,2,1,0:T(8,128)} %copy.47), kind=kLoop, calls=%fused_computation.118 | loop fusion | flops 83200 | bytes 1497600 | tf_op jit(solution)/shard_map/concatenate | solution.py:28
  119.3 2.1 collective-permute-start.8
  121.4 2.6 collective-permute-start.9
  124.2 3.8 %collective-permute-done.9 = f32[5,32,1,130]{3,2,1,0:T(1,128)S(1)} collective-permute-done((f32[5,32,1,130]{3,2,1,0:T(1,128)S(1)}, f32[5,32,1,130]{3,2,1,0:T(1,128)S(1)}, u32[]{:S(2)}, u32[]{:S(2)}) %collective-permute-start.9) | collective-permute-done | bytes 83232 | tf_op jit(solution)/shard_map/ppermute | solution.py:24
  129.5 5.0 %collective-permute-start.11 = (f32[5,1,18,130]{3,2,1,0:T(8,128)S(1)}, f32[5,1,18,130]{3,2,1,0:T(8,128)S(1)}, u32[]{:S(2)}, u32[]{:S(2)}) collective-permute-start(f32[5,1,18,130]{3,2,1,0:T(8,128)S(1)} %get-tuple-element.69), channel_id=1, source_target_pairs={{0,1},{1,2},{2,3},{4,5},{5,6},{6,7},{8,9},{9,10},{10,11},{12,13},{... | collective-permute-start | bytes 140408 | tf_op jit(solution)/shard_map/ppermute | solution.py:24
  136.9 3.1 %broadcast_multiply_fusion = (f32[5,32,16,128]{3,2,1,0:T(8,128)S(1)}, f32[5,32,16,128]{3,2,1,0:T(8,128)S(1)}) fusion(f32[5,1,18,130]{3,2,1,0:T(8,128)S(1)} %collective-permute-done.10, f32[5,32,1,130]{3,2,1,0:T(1,128)S(1)} %collective-permute-done.8, f32[5,32,16,1]{3,2,1,0:T(8,128)S(1)} %copy-done.4, f32[5,32,16,128]{3,2,1,0:T(8,128)S(1)} %multiply_add_fusion, ...), kind=kLoop, calls=%fused_computation.47 | loop fusion | flops 5242880 | bytes 4212640 | tf_op jit(solution)/shard_map/mul | solution.py:59
  140.4 5.0 %add_multiply_fusion = f32[5,32,16,128]{3,2,1,0:T(8,128)S(1)} fusion(f32[5,32,16,128]{3,2,1,0:T(8,128)S(1)} %broadcast_dynamic-update-slice_fusion, f32[5,32,16,128]{3,2,1,0:T(8,128)S(1)} %multiply_add_fusion, f32[5,32,16,128]{3,2,1,0:T(8,128)S(1)} %copy-done.1, f32[32,16,128]{2,1,0:T(8,128)S(1)} %get-tuple-element.82, ...), kind=kLoop, calls=%fused_computation.44 | loop fusion | flops 14090240 | bytes 6320564 | tf_op jit(solution)/shard_map/mul | solution.py:157
  146.5 11.8 %gather_fusion = f32[2048]{0:T(1024)S(1)} fusion(f32[65536]{0:T(1024)S(1)} %bitcast.150, s32[2048]{0:T(1024)S(1)} %broadcast_clamp_fusion), kind=kCustom, calls=%fused_computation | custom fusion | bytes 24576 | tf_op jit(solution)/shard_map/gather | solution.py:159
  158.2 16.8 %all-gather = f32[32768]{0:T(1024)S(1)} all-gather(f32[2048]{0:T(1024)S(1)} %gather_fusion), channel_id=2, replica_groups=mesh['stream'=8,'span'=16,'vert'=4] {'span'}, dimensions={0}, use_global_device_ids=true | all-gather | bytes 139264 | tf_op jit(solution)/shard_map/all_gather | solution.py:161
  175.2 10.6 %while.11 = (s32[]{:T(128)}, f32[3,64]{1,0:T(4,128)S(1)}, f32[16,3,2048]{2,0,1:T(8,128)S(1)}, s32[16,2048]{1,0:T(8,128)S(1)}, s32[]{:T(128)}, /*index=5*/s32[]{:T(128)}) while((s32[]{:T(128)}, f32[3,64]{1,0:T(4,128)S(1)}, f32[16,3,2048]{2,0,1:T(8,128)S(1)}, s32[16,2048]{1,0:T(8,128)S(1)}, s32[]{:T(128)}, /*index=5*/s32[]{:T(128)}) %tuple.46), condition=%wide.region_5.6_spmd.clone, body=%wide.region_4.5_spmd.clone.sunk | while | flops 4850051 | bytes 99927 | solution.py:104
  186.0 77.3 %psum.15 = f32[32]{0:T(128)} all-reduce(f32[32]{0:T(128)S(1)} %convolution_bitcast_fusion), channel_id=1, replica_groups=mesh['stream'=8,'span'=16,'vert'=4] {'stream','vert'}, use_global_device_ids=true, to_apply=%region_6.7 | all-reduce | flops 32 | bytes 256 | tf_op jit(solution)/shard_map/psum | solution.py:165
  (152 shorter events, 46.9 us)
Async XLA Ops:
  0.6 185.2 %copy-start = (f32[3,64,32]{1,2,0:T(8,128)S(1)}, f32[3,64,32]{1,2,0:T(8,128)}, u32[]{:S(2)}) copy-start(f32[3,64,32]{1,2,0:T(8,128)} %param.20) | copy-start | bytes 73732
  3.4 25.0 %collective-permute-start = (f32[5,32,16,1]{1,2,3,0:T(8,128)S(1)}, f32[5,32,16,1]{1,2,3,0:T(8,128)S(1)}, u32[]{:S(2)}, u32[]{:S(2)}) collective-permute-start(f32[5,32,16,1]{1,2,3,0:T(8,128)S(1)} %copy.55), channel_id=1, source_target_pairs={{64,0},{128,64},{192,128},{256,192},{320,256},{384,320},{448,384},... | collective-permute-start | bytes 30728 | tf_op jit(solution)/shard_map/ppermute | solution.py:27
  5.3 23.7 %collective-permute-start.1 = (f32[5,32,16,1]{1,2,3,0:T(8,128)S(1)}, f32[5,32,16,1]{1,2,3,0:T(8,128)S(1)}, u32[]{:S(2)}, u32[]{:S(2)}) collective-permute-start(f32[5,32,16,1]{1,2,3,0:T(8,128)S(1)} %copy.56), channel_id=1, source_target_pairs={{0,64},{64,128},{128,192},{192,256},{256,320},{320,384},{384,448},... | collective-permute-start | bytes 30728 | tf_op jit(solution)/shard_map/ppermute | solution.py:24
  10.7 14.8 %copy-start.1 = (f32[5,32,16,128]{3,2,1,0:T(8,128)S(1)}, f32[5,32,16,128]{3,2,1,0:T(8,128)}, u32[]{:S(2)}) copy-start(f32[5,32,16,128]{3,2,1,0:T(8,128)} %param.13) | copy-start | bytes 3932164
  12.2 14.2 %copy-start.13 = (s32[1,1,1,2048]{3,2,1,0:T(1,128)S(1)}, s32[1,1,1,2048]{3,2,1,0:T(1,128)}, u32[]{:S(2)}) copy-start(s32[1,1,1,2048]{3,2,1,0:T(1,128)} %param.17) | copy-start | bytes 24580
  12.2 46.5 %all-to-all-start = ((f32[64,1,2560]{2,1,0:T(1,128)}), f32[64,1,2560]{2,1,0:T(1,128)}, u32[]{:S(2)}, u32[]{:S(2)}) async-start(f32[64,1,2560]{2,1,0:T(1,128)} %all_to_all.8), calls=%async_computation | async-start | bytes 1310720 | tf_op jit(solution)/shard_map/all_to_all | solution.py:128
  29.1 22.7 %copy-start.2 = (f32[5,32,16,1]{3,2,1,0:T(8,128)}, f32[5,32,16,1]{3,2,1,0:T(8,128)S(1)}, u32[]{:S(2)}) copy-start(f32[5,32,16,1]{3,2,1,0:T(8,128)S(1)} %copy.37) | copy-start | bytes 30724
  30.7 12.4 %copy-start.3 = (f32[5,32,16,1]{3,2,1,0:T(8,128)S(1)}, f32[5,32,16,1]{3,2,1,0:T(8,128)}, u32[]{:S(2)}) copy-start(f32[5,32,16,1]{3,2,1,0:T(8,128)} %copy.39) | copy-start | bytes 30724
  33.2 8.4 %collective-permute-start.2 = (f32[5,32,1,130]{3,2,1,0:T(1,128)S(1)}, f32[5,32,1,130]{3,2,1,0:T(1,128)S(1)}, u32[]{:S(2)}, u32[]{:S(2)}) collective-permute-start(f32[5,32,1,130]{3,2,1,0:T(1,128)S(1)} %get-tuple-element.80), channel_id=1, source_target_pairs={{4,0},{8,4},{12,8},{16,12},{20,16},{24,20},{28,24},{32,28},{36,32}... | collective-permute-start | bytes 249608 | tf_op jit(solution)/shard_map/ppermute | solution.py:27
  35.2 7.9 %collective-permute-start.3 = (f32[5,32,1,130]{3,2,1,0:T(1,128)S(1)}, f32[5,32,1,130]{3,2,1,0:T(1,128)S(1)}, u32[]{:S(2)}, u32[]{:S(2)}) collective-permute-start(f32[5,32,1,130]{3,2,1,0:T(1,128)S(1)} %get-tuple-element.79), channel_id=1, source_target_pairs={{0,4},{4,8},{8,12},{12,16},{16,20},{20,24},{24,28},{28,32},{32,36}... | collective-permute-start | bytes 249608 | tf_op jit(solution)/shard_map/ppermute | solution.py:24
  43.2 7.3 %collective-permute-start.4 = (f32[5,1,18,130]{3,2,1,0:T(8,128)S(1)}, f32[5,1,18,130]{3,2,1,0:T(8,128)S(1)}, u32[]{:S(2)}, u32[]{:S(2)}) collective-permute-start(f32[5,1,18,130]{3,2,1,0:T(8,128)S(1)} %get-tuple-element.72), channel_id=1, source_target_pairs={{1,0},{2,1},{3,2},{5,4},{6,5},{7,6},{9,8},{10,9},{11,10},{13,12},{... | collective-permute-start | bytes 140408 | tf_op jit(solution)/shard_map/ppermute | solution.py:27
  44.5 7.2 %collective-permute-start.5 = (f32[5,1,18,130]{3,2,1,0:T(8,128)S(1)}, f32[5,1,18,130]{3,2,1,0:T(8,128)S(1)}, u32[]{:S(2)}, u32[]{:S(2)}) collective-permute-start(f32[5,1,18,130]{3,2,1,0:T(8,128)S(1)} %get-tuple-element.71), channel_id=1, source_target_pairs={{0,1},{1,2},{2,3},{4,5},{5,6},{6,7},{8,9},{9,10},{10,11},{12,13},{... | collective-permute-start | bytes 140408 | tf_op jit(solution)/shard_map/ppermute | solution.py:24
  61.3 32.6 %copy-start.16 = (f32[5]{0:T(128)S(1)}, f32[5]{0:T(128)}, u32[]{:S(2)}) copy-start(f32[5]{0:T(128)} %constant.116.clone) | copy-start | bytes 64
  61.4 32.6 %copy-start.15 = (f32[5]{0:T(128)S(1)}, f32[5]{0:T(128)}, u32[]{:S(2)}) copy-start(f32[5]{0:T(128)} %constant.117.clone) | copy-start | bytes 64
  103.5 9.7 %copy-start.12 = (s32[1,16,1,2048]{3,2,1,0:T(1,128)S(1)}, s32[1,16,1,2048]{3,2,1,0:T(1,128)}, u32[]{:S(2)}) copy-start(s32[1,16,1,2048]{3,2,1,0:T(1,128)} %param.19) | copy-start | bytes 393220
  105.4 7.8 %collective-permute-start.6 = (f32[5,32,16,1]{1,2,3,0:T(8,128)S(1)}, f32[5,32,16,1]{1,2,3,0:T(8,128)S(1)}, u32[]{:S(2)}, u32[]{:S(2)}) collective-permute-start(f32[5,32,16,1]{1,2,3,0:T(8,128)S(1)} %copy.44), channel_id=1, source_target_pairs={{64,0},{128,64},{192,128},{256,192},{320,256},{384,320},{448,384},... | collective-permute-start | bytes 30728 | tf_op jit(solution)/shard_map/ppermute | solution.py:27
  108.5 6.3 %collective-permute-start.7 = (f32[5,32,16,1]{1,2,3,0:T(8,128)S(1)}, f32[5,32,16,1]{1,2,3,0:T(8,128)S(1)}, u32[]{:S(2)}, u32[]{:S(2)}) collective-permute-start(f32[5,32,16,1]{1,2,3,0:T(8,128)S(1)} %copy.46), channel_id=1, source_target_pairs={{0,64},{64,128},{128,192},{192,256},{256,320},{320,384},{384,448},... | collective-permute-start | bytes 30728 | tf_op jit(solution)/shard_map/ppermute | solution.py:24
  116.4 11.6 %copy-start.5 = (f32[5,32,16,1]{3,2,1,0:T(8,128)S(1)}, f32[5,32,16,1]{3,2,1,0:T(8,128)}, u32[]{:S(2)}) copy-start(f32[5,32,16,1]{3,2,1,0:T(8,128)} %copy.47) | copy-start | bytes 30724
  119.3 8.7 %copy-start.4 = (f32[5,32,16,1]{3,2,1,0:T(8,128)S(1)}, f32[5,32,16,1]{3,2,1,0:T(8,128)}, u32[]{:S(2)}) copy-start(f32[5,32,16,1]{3,2,1,0:T(8,128)} %copy.45) | copy-start | bytes 30724
  119.3 4.9 %collective-permute-start.8 = (f32[5,32,1,130]{3,2,1,0:T(1,128)S(1)}, f32[5,32,1,130]{3,2,1,0:T(1,128)S(1)}, u32[]{:S(2)}, u32[]{:S(2)}) collective-permute-start(f32[5,32,1,130]{3,2,1,0:T(1,128)S(1)} %get-tuple-element.76), channel_id=1, source_target_pairs={{4,0},{8,4},{12,8},{16,12},{20,16},{24,20},{28,24},{32,28},{36,32}... | collective-permute-start | bytes 249608 | tf_op jit(solution)/shard_map/ppermute | solution.py:27
  121.4 6.6 %collective-permute-start.9 = (f32[5,32,1,130]{3,2,1,0:T(1,128)S(1)}, f32[5,32,1,130]{3,2,1,0:T(1,128)S(1)}, u32[]{:S(2)}, u32[]{:S(2)}) collective-permute-start(f32[5,32,1,130]{3,2,1,0:T(1,128)S(1)} %get-tuple-element.75), channel_id=1, source_target_pairs={{0,4},{4,8},{8,12},{12,16},{16,20},{20,24},{24,28},{28,32},{32,36}... | collective-permute-start | bytes 249608 | tf_op jit(solution)/shard_map/ppermute | solution.py:24
  128.2 7.4 %collective-permute-start.10 = (f32[5,1,18,130]{3,2,1,0:T(8,128)S(1)}, f32[5,1,18,130]{3,2,1,0:T(8,128)S(1)}, u32[]{:S(2)}, u32[]{:S(2)}) collective-permute-start(f32[5,1,18,130]{3,2,1,0:T(8,128)S(1)} %get-tuple-element.70), channel_id=1, source_target_pairs={{1,0},{2,1},{3,2},{5,4},{6,5},{7,6},{9,8},{10,9},{11,10},{13,12},{... | collective-permute-start | bytes 140408 | tf_op jit(solution)/shard_map/ppermute | solution.py:27
  129.5 7.4 %collective-permute-start.11 = (f32[5,1,18,130]{3,2,1,0:T(8,128)S(1)}, f32[5,1,18,130]{3,2,1,0:T(8,128)S(1)}, u32[]{:S(2)}, u32[]{:S(2)}) collective-permute-start(f32[5,1,18,130]{3,2,1,0:T(8,128)S(1)} %get-tuple-element.69), channel_id=1, source_target_pairs={{0,1},{1,2},{2,3},{4,5},{5,6},{6,7},{8,9},{9,10},{10,11},{12,13},{... | collective-permute-start | bytes 140408 | tf_op jit(solution)/shard_map/ppermute | solution.py:24
  146.4 28.6 %copy-start.10 = (f32[1,16,1,3,2048]{4,2,3,1,0:T(1,128)S(1)}, f32[1,16,1,3,2048]{4,2,3,1,0:T(1,128)}, u32[]{:S(2)}) copy-start(f32[1,16,1,3,2048]{4,2,3,1,0:T(1,128)} %param.18) | copy-start | bytes 1179652
  (6 other events, 27.6 us)
where the time goes:
time: 264 us; the launch traced here: 263 us
  blocking collectives  125 us (47%)
  starting transfers between devices  46.3 us (18%)
  other arithmetic  36.1 us (14%)
  local copies, waits for them, and re-layouts  30.7 us (12%)
  waiting for transfers between devices  12.1 us (5%)
  matrix products  11.3 us (4%)
    psum x1, blocking collectives, on_device(): modal_force = lax.psum(modal_part, ('stream', 'vert'))  77.3 us
    psum x1, blocking collectives, on_device(): lax.psum(partial_value, 'stream').reshape(5, depth_cells, span_cells)  30.8 us
    ppermute x6, starting transfers between devices, extended(): lax.ppermute(lax.slice_in_dim(block, block.shape[dim] - width, None, axis...  23.8 us
    all_gather x1, blocking collectives, on_device(): lax.all_gather(sampled.reshape(1, 1, 1, -1), 'span', axis=1, tiled=True)  16.8 us
    all_to_all x1, starting transfers between devices, on_device(): lax.all_to_all(outgoing.reshape(tile_count, CAP * 5 * spec_cols), ('span'...  13.3 us
    gather x1, local copies, waits for them, and re-layouts, on_device(): sampled = pressure[deck_cells[0, 0, 0]]  11.8 us
    dot_general x16, matrix products, add_row(): jnp.dot(row_values, member, precision=lax.Precision.HIGHEST)  9.31 us
    ppermute x6, starting transfers between devices, extended(): lax.ppermute(lax.slice_in_dim(block, 0, width, axis=dim), axis, backward)  9.23 us
  transfers between devices with their start and end apart: 13, of which 7 were waited for; matrix products, arithmetic and copies ran while one was open for 8% of the time, Pallas kernels for 0%

commit v1 on v0

--- a/solution.py
+++ b/solution.py
@@ -14,6 +14,27 @@
 relax_time = 0.5
 relax_depth = 8.0
 wave_cols = 16
+
+
+def collect(x, axis, dim):
+    size, index, rows = (lax.axis_size(axis), lax.axis_index(axis), x.shape[dim])
+    forward = [(i, (i + 1) % size) for i in range(size)]
+    downward = [(i, (i - 1) % size) for i in range(size)]
+    out = jnp.zeros((*x.shape[:dim], size * rows, *x.shape[dim + 1 :]), x.dtype)
+    out = lax.dynamic_update_slice_in_dim(out, x, index * rows, axis=dim)
+    from_left = from_right = x
+    half = size // 2
+    for step in range(1, half + 1):
+        from_left = lax.ppermute(from_left, axis, forward)
+        out = lax.dynamic_update_slice_in_dim(
+            out, from_left, (index - step) % size * rows, axis=dim
+        )
+        if step < size - half:
+            from_right = lax.ppermute(from_right, axis, downward)
+            out = lax.dynamic_update_slice_in_dim(
+                out, from_right, (index + step) % size * rows, axis=dim
+            )
+    return out
 
 
 def extended(block, sides, width):
@@ -158,7 +179,7 @@
     pressure = new_fields[3].reshape(-1)
     sampled = pressure[deck_cells[0, 0, 0]]
     strip_count = mode_shapes.shape[1]
-    rows_all = lax.all_gather(sampled.reshape(1, 1, 1, -1), "span", axis=1, tiled=True)
+    rows_all = collect(sampled.reshape(1, 1, 1, -1), "span", 1)
     traction = rows_all[0, :, 0][:, None, :] * deck_geom[0, :, 0]
     forces = strip_forces(traction, strip_ids[0, :, 0], strip_count)
     modal_part = jnp.einsum("cj,cjm->m", forces, mode_shapes, precision=lax.Precision.HIGHEST)

time: 264 us -> 278 us (1.053)
  the two profiles are of different devices: /device:TPU:64 before, /device:TPU:256 now
where the time goes in v1:
time: 278 us; the launch traced here: 277 us
  blocking collectives  108 us (39%)
  starting transfers between devices  64.1 us (23%)
  local copies, waits for them, and re-layouts  34.3 us (12%)
  other arithmetic  33.3 us (12%)
  waiting for transfers between devices  23.7 us (9%)
  matrix products  11.3 us (4%)
    psum x1, blocking collectives, on_device(): modal_force = lax.psum(modal_part, ('stream', 'vert'))  77.4 us
    psum x1, blocking collectives, on_device(): lax.psum(partial_value, 'stream').reshape(5, depth_cells, span_cells)  30.8 us
    ppermute x6, starting transfers between devices, extended(): lax.ppermute(lax.slice_in_dim(block, block.shape[dim] - width, None, axis...  23.6 us
    ppermute x7, starting transfers between devices, collect(): from_right = lax.ppermute(from_right, axis, downward)  20.5 us
    gather x1, local copies, waits for them, and re-layouts, on_device(): sampled = pressure[deck_cells[0, 0, 0]]  11.8 us
    all_to_all x1, starting transfers between devices, on_device(): lax.all_to_all(outgoing.reshape(tile_count, CAP * 5 * spec_cols), ('span'...  10.7 us
    ppermute x8, waiting for transfers between devices, collect(): from_left = lax.ppermute(from_left, axis, forward)  10.2 us
    ppermute x6, starting transfers between devices, extended(): lax.ppermute(lax.slice_in_dim(block, 0, width, axis=dim), axis, backward)  9.38 us
  transfers between devices with their start and end apart: 28, of which 14 were waited for; matrix products, arithmetic and copies ran while one was open for 8% of the time, Pallas kernels for 0%

profile of v1, /device:TPU:256, one launch (start us, length us, event | category | flops | bytes accessed | tf_op | source)
XLA Modules:
  0.0 277.0 jit_solution(17347569069101850310)
XLA Ops:
  5.3 4.5 %collective-permute-start.1 = (f32[5,32,16,1]{1,2,3,0:T(8,128)S(1)}, f32[5,32,16,1]{1,2,3,0:T(8,128)S(1)}, u32[]{:S(2)}, u32[]{:S(2)}) collective-permute-start(f32[5,32,16,1]{1,2,3,0:T(8,128)S(1)} %copy.56), channel_id=1, source_target_pairs={{0,64},{64,128},{128,192},{192,256},{256,320},{320,384},{384,448},... | collective-permute-start | bytes 30728 | tf_op jit(solution)/shard_map/ppermute | solution.py:45
  12.2 10.7 %all-to-all-start = ((f32[64,1,2560]{2,1,0:T(1,128)}), f32[64,1,2560]{2,1,0:T(1,128)}, u32[]{:S(2)}, u32[]{:S(2)}) async-start(f32[64,1,2560]{2,1,0:T(1,128)} %all_to_all.8), calls=%async_computation | async-start | bytes 1310720 | tf_op jit(solution)/shard_map/all_to_all | solution.py:149
  34.9 4.0 %collective-permute-done.2 = f32[5,32,1,130]{3,2,1,0:T(1,128)S(1)} collective-permute-done((f32[5,32,1,130]{3,2,1,0:T(1,128)S(1)}, f32[5,32,1,130]{3,2,1,0:T(1,128)S(1)}, u32[]{:S(2)}, u32[]{:S(2)}) %collective-permute-start.2) | collective-permute-done | bytes 83232 | tf_op jit(solution)/shard_map/ppermute | solution.py:48
  42.1 4.7 %collective-permute-start.5 = (f32[5,1,18,130]{3,2,1,0:T(8,128)S(1)}, f32[5,1,18,130]{3,2,1,0:T(8,128)S(1)}, u32[]{:S(2)}, u32[]{:S(2)}) collective-permute-start(f32[5,1,18,130]{3,2,1,0:T(8,128)S(1)} %get-tuple-element.71), channel_id=1, source_target_pairs={{0,1},{1,2},{2,3},{4,5},{5,6},{6,7},{8,9},{9,10},{10,11},{12,13},{... | collective-permute-start | bytes 140408 | tf_op jit(solution)/shard_map/ppermute | solution.py:45
  49.0 3.2 %broadcast_multiply_fusion.3 = (f32[5,32,16,128]{3,2,1,0:T(8,128)S(1)}, f32[5,32,16,128]{3,2,1,0:T(8,128)S(1)}) fusion(f32[5,1,18,130]{3,2,1,0:T(8,128)S(1)} %collective-permute-done.4, f32[5,32,1,130]{3,2,1,0:T(1,128)S(1)} %collective-permute-done.2, f32[5,32,16,1]{3,2,1,0:T(8,128)S(1)} %copy.37, f32[5,32,16,128]{3,2,1,0:T(8,128)S(1)} %copy-done.1, ...), kind=kLoop, calls=%fused_computation.50 | loop fusion | flops 5242880 | bytes 4212640 | tf_op jit(solution)/shard_map/mul | solution.py:80
  53.6 2.6 reduce
  58.1 30.8 %psum.14 = f32[5,32,16]{2,1,0:T(8,128)S(1)} all-reduce(f32[5,32,16]{2,1,0:T(8,128)S(1)} %reshape.280), channel_id=1, replica_groups=mesh['stream'=8,'span'=16,'vert'=4] {'stream'}, use_global_device_ids=true, to_apply=%region_3.4 | all-reduce | flops 2560 | bytes 20480 | tf_op jit(solution)/shard_map/psum | solution.py:165
  88.9 7.5 %multiply_add_fusion = f32[5,32,16,128]{3,2,1,0:T(8,128)S(1)} fusion(f32[5,32,16,128]{3,2,1,0:T(8,128)S(1)} %copy-done.1, f32[5,32,16,128]{3,2,1,0:T(8,128)} %copy-done.8, f32[5,32,16]{2,1,0:T(8,128)S(1)} %broadcast_add_fusion.1, f32[128]{0:T(128)S(1)} %compare_select_fusion.1, f32[32,16,128]{2,1,0:T(8,128)} %get-tuple-element.87, ...), kind=kLoop, calls=%fused_computation.45 | loop fusion | flops 13434880 | bytes 5009844 | tf_op jit(solution)/shard_map/add | solution.py:176
  103.4 4.5 %collective-permute-start.7 = (f32[5,32,16,1]{1,2,3,0:T(8,128)S(1)}, f32[5,32,16,1]{1,2,3,0:T(8,128)S(1)}, u32[]{:S(2)}, u32[]{:S(2)}) collective-permute-start(f32[5,32,16,1]{1,2,3,0:T(8,128)S(1)} %copy.46), channel_id=1, source_target_pairs={{0,64},{64,128},{128,192},{192,256},{256,320},{320,384},{384,448},... | collective-permute-start | bytes 30728 | tf_op jit(solution)/shard_map/ppermute | solution.py:45
  111.3 2.9 %pad_maximum_fusion.36 = (f32[5,32,1,130]{3,2,1,0:T(1,128)S(1)}, f32[5,32,1,130]{3,2,1,0:T(1,128)S(1)}) fusion(f32[5,32,16,1]{3,2,1,0:T(8,128)} %copy.45, f32[5,32,16,128]{3,2,1,0:T(8,128)S(1)} %multiply_add_fusion, f32[5,32,16,1]{3,2,1,0:T(8,128)} %copy.47), kind=kLoop, calls=%fused_computation.118 | loop fusion | flops 83200 | bytes 1497600 | tf_op jit(solution)/shard_map/concatenate | solution.py:49
  119.0 5.0 %collective-permute-done.9 = f32[5,32,1,130]{3,2,1,0:T(1,128)S(1)} collective-permute-done((f32[5,32,1,130]{3,2,1,0:T(1,128)S(1)}, f32[5,32,1,130]{3,2,1,0:T(1,128)S(1)}, u32[]{:S(2)}, u32[]{:S(2)}) %collective-permute-start.9) | collective-permute-done | bytes 83232 | tf_op jit(solution)/shard_map/ppermute | solution.py:45
  125.5 5.0 %collective-permute-start.11 = (f32[5,1,18,130]{3,2,1,0:T(8,128)S(1)}, f32[5,1,18,130]{3,2,1,0:T(8,128)S(1)}, u32[]{:S(2)}, u32[]{:S(2)}) collective-permute-start(f32[5,1,18,130]{3,2,1,0:T(8,128)S(1)} %get-tuple-element.69), channel_id=1, source_target_pairs={{0,1},{1,2},{2,3},{4,5},{5,6},{6,7},{8,9},{9,10},{10,11},{12,13},{... | collective-permute-start | bytes 140408 | tf_op jit(solution)/shard_map/ppermute | solution.py:45
  132.9 3.1 %broadcast_multiply_fusion = (f32[5,32,16,128]{3,2,1,0:T(8,128)S(1)}, f32[5,32,16,128]{3,2,1,0:T(8,128)S(1)}) fusion(f32[5,1,18,130]{3,2,1,0:T(8,128)S(1)} %collective-permute-done.10, f32[5,32,1,130]{3,2,1,0:T(1,128)S(1)} %collective-permute-done.8, f32[5,32,16,1]{3,2,1,0:T(8,128)S(1)} %copy-done.4, f32[5,32,16,128]{3,2,1,0:T(8,128)S(1)} %multiply_add_fusion, ...), kind=kLoop, calls=%fused_computation.47 | loop fusion | flops 5242880 | bytes 4212640 | tf_op jit(solution)/shard_map/mul | solution.py:80
  136.4 5.0 %add_multiply_fusion = f32[5,32,16,128]{3,2,1,0:T(8,128)S(1)} fusion(f32[5,32,16,128]{3,2,1,0:T(8,128)S(1)} %broadcast_dynamic-update-slice_fusion, f32[5,32,16,128]{3,2,1,0:T(8,128)S(1)} %multiply_add_fusion, f32[5,32,16,128]{3,2,1,0:T(8,128)S(1)} %copy-done.1, f32[32,16,128]{2,1,0:T(8,128)S(1)} %get-tuple-element.82, ...), kind=kLoop, calls=%fused_computation.44 | loop fusion | flops 14090240 | bytes 6320564 | tf_op jit(solution)/shard_map/mul | solution.py:178
  142.5 11.8 %gather_fusion = f32[2048]{0:T(1024)S(1)} fusion(f32[65536]{0:T(1024)S(1)} %bitcast.167, s32[2048]{0:T(1024)S(1)} %broadcast_clamp_fusion), kind=kCustom, calls=%fused_computation | custom fusion | bytes 24576 | tf_op jit(solution)/shard_map/gather | solution.py:180
  154.3 2.9 %collective-permute-start.13 = (f32[1,1,1,2048]{3,2,1,0:T(1,128)S(1)}, f32[1,1,1,2048]{3,2,1,0:T(1,128)S(1)}, u32[]{:S(2)}, u32[]{:S(2)}) collective-permute-start(f32[1,1,1,2048]{3,2,1,0:T(1,128)S(1)} %bitcast.174), channel_id=1, source_target_pairs={{0,60},{4,0},{8,4},{12,8},{16,12},{20,16},{24,20},{28,24},{32,28},... | collective-permute-start | bytes 24584 | tf_op jit(solution)/shard_map/ppermute | solution.py:33
  158.6 2.9 %collective-permute-start.15 = (f32[1,1,1,2048]{3,2,1,0:T(1,128)S(1)}, f32[1,1,1,2048]{3,2,1,0:T(1,128)S(1)}, u32[]{:S(2)}, u32[]{:S(2)}) collective-permute-start(f32[1,1,1,2048]{3,2,1,0:T(1,128)S(1)} %collective-permute-done.13), channel_id=1, source_target_pairs={{0,60},{4,0},{8,4},{12,8},{16,12},{20,16},{24,20},{28,24},{32,28},... | collective-permute-start | bytes 24584 | tf_op jit(solution)/shard_map/ppermute | solution.py:33
  162.9 2.9 %collective-permute-start.17 = (f32[1,1,1,2048]{3,2,1,0:T(1,128)S(1)}, f32[1,1,1,2048]{3,2,1,0:T(1,128)S(1)}, u32[]{:S(2)}, u32[]{:S(2)}) collective-permute-start(f32[1,1,1,2048]{3,2,1,0:T(1,128)S(1)} %collective-permute-done.15), channel_id=1, source_target_pairs={{0,60},{4,0},{8,4},{12,8},{16,12},{20,16},{24,20},{28,24},{32,28},... | collective-permute-start | bytes 24584 | tf_op jit(solution)/shard_map/ppermute | solution.py:33
  167.2 2.9 %collective-permute-start.19 = (f32[1,1,1,2048]{3,2,1,0:T(1,128)S(1)}, f32[1,1,1,2048]{3,2,1,0:T(1,128)S(1)}, u32[]{:S(2)}, u32[]{:S(2)}) collective-permute-start(f32[1,1,1,2048]{3,2,1,0:T(1,128)S(1)} %collective-permute-done.17), channel_id=1, source_target_pairs={{0,60},{4,0},{8,4},{12,8},{16,12},{20,16},{24,20},{28,24},{32,28},... | collective-permute-start | bytes 24584 | tf_op jit(solution)/shard_map/ppermute | solution.py:33
  171.5 2.9 %collective-permute-start.21 = (f32[1,1,1,2048]{3,2,1,0:T(1,128)S(1)}, f32[1,1,1,2048]{3,2,1,0:T(1,128)S(1)}, u32[]{:S(2)}, u32[]{:S(2)}) collective-permute-start(f32[1,1,1,2048]{3,2,1,0:T(1,128)S(1)} %collective-permute-done.19), channel_id=1, source_target_pairs={{0,60},{4,0},{8,4},{12,8},{16,12},{20,16},{24,20},{28,24},{32,28},... | collective-permute-start | bytes 24584 | tf_op jit(solution)/shard_map/ppermute | solution.py:33
  175.7 2.9 %collective-permute-start.23 = (f32[1,1,1,2048]{3,2,1,0:T(1,128)S(1)}, f32[1,1,1,2048]{3,2,1,0:T(1,128)S(1)}, u32[]{:S(2)}, u32[]{:S(2)}) collective-permute-start(f32[1,1,1,2048]{3,2,1,0:T(1,128)S(1)} %collective-permute-done.21), channel_id=1, source_target_pairs={{0,60},{4,0},{8,4},{12,8},{16,12},{20,16},{24,20},{28,24},{32,28},... | collective-permute-start | bytes 24584 | tf_op jit(solution)/shard_map/ppermute | solution.py:33
  180.0 2.9 %collective-permute-start.25 = (f32[1,1,1,2048]{3,2,1,0:T(1,128)S(1)}, f32[1,1,1,2048]{3,2,1,0:T(1,128)S(1)}, u32[]{:S(2)}, u32[]{:S(2)}) collective-permute-start(f32[1,1,1,2048]{3,2,1,0:T(1,128)S(1)} %collective-permute-done.23), channel_id=1, source_target_pairs={{0,60},{4,0},{8,4},{12,8},{16,12},{20,16},{24,20},{28,24},{32,28},... | collective-permute-start | bytes 24584 | tf_op jit(solution)/shard_map/ppermute | solution.py:33
  188.9 10.6 %while.11 = (s32[]{:T(128)}, f32[3,64]{1,0:T(4,128)S(1)}, f32[16,3,2048]{2,0,1:T(8,128)S(1)}, s32[16,2048]{1,0:T(8,128)S(1)}, s32[]{:T(128)}, /*index=5*/s32[]{:T(128)}) while((s32[]{:T(128)}, f32[3,64]{1,0:T(4,128)S(1)}, f32[16,3,2048]{2,0,1:T(8,128)S(1)}, s32[16,2048]{1,0:T(8,128)S(1)}, s32[]{:T(128)}, /*index=5*/s32[]{:T(128)}) %tuple.46), condition=%wide.region_5.6_spmd.clone, body=%wide.region_4.5_spmd.clone.sunk | while | flops 4850051 | bytes 99927 | solution.py:125
  199.7 77.4 %psum.15 = f32[32]{0:T(128)} all-reduce(f32[32]{0:T(128)S(1)} %convolution_bitcast_fusion), channel_id=1, replica_groups=mesh['stream'=8,'span'=16,'vert'=4] {'stream','vert'}, use_global_device_ids=true, to_apply=%region_6.7 | all-reduce | flops 32 | bytes 256 | tf_op jit(solution)/shard_map/psum | solution.py:186
  (199 shorter events, 71.7 us)
Async XLA Ops:
  3.4 22.4 %collective-permute-start = (f32[5,32,16,1]{1,2,3,0:T(8,128)S(1)}, f32[5,32,16,1]{1,2,3,0:T(8,128)S(1)}, u32[]{:S(2)}, u32[]{:S(2)}) collective-permute-start(f32[5,32,16,1]{1,2,3,0:T(8,128)S(1)} %copy.55), channel_id=1, source_target_pairs={{64,0},{128,64},{192,128},{256,192},{320,256},{384,320},{448,384},... | collective-permute-start | bytes 30728 | tf_op jit(solution)/shard_map/ppermute | solution.py:48
  5.3 21.1 %collective-permute-start.1 = (f32[5,32,16,1]{1,2,3,0:T(8,128)S(1)}, f32[5,32,16,1]{1,2,3,0:T(8,128)S(1)}, u32[]{:S(2)}, u32[]{:S(2)}) collective-permute-start(f32[5,32,16,1]{1,2,3,0:T(8,128)S(1)} %copy.56), channel_id=1, source_target_pairs={{0,64},{64,128},{128,192},{192,256},{256,320},{320,384},{384,448},... | collective-permute-start | bytes 30728 | tf_op jit(solution)/shard_map/ppermute | solution.py:45
  12.2 41.4 %all-to-all-start = ((f32[64,1,2560]{2,1,0:T(1,128)}), f32[64,1,2560]{2,1,0:T(1,128)}, u32[]{:S(2)}, u32[]{:S(2)}) async-start(f32[64,1,2560]{2,1,0:T(1,128)} %all_to_all.8), calls=%async_computation | async-start | bytes 1310720 | tf_op jit(solution)/shard_map/all_to_all | solution.py:149
  30.6 8.4 %collective-permute-start.2 = (f32[5,32,1,130]{3,2,1,0:T(1,128)S(1)}, f32[5,32,1,130]{3,2,1,0:T(1,128)S(1)}, u32[]{:S(2)}, u32[]{:S(2)}) collective-permute-start(f32[5,32,1,130]{3,2,1,0:T(1,128)S(1)} %get-tuple-element.80), channel_id=1, source_target_pairs={{4,0},{8,4},{12,8},{16,12},{20,16},{24,20},{28,24},{32,28},{36,32}... | collective-permute-start | bytes 249608 | tf_op jit(solution)/shard_map/ppermute | solution.py:48
  32.7 7.8 %collective-permute-start.3 = (f32[5,32,1,130]{3,2,1,0:T(1,128)S(1)}, f32[5,32,1,130]{3,2,1,0:T(1,128)S(1)}, u32[]{:S(2)}, u32[]{:S(2)}) collective-permute-start(f32[5,32,1,130]{3,2,1,0:T(1,128)S(1)} %get-tuple-element.79), channel_id=1, source_target_pairs={{0,4},{4,8},{8,12},{12,16},{16,20},{20,24},{24,28},{28,32},{32,36}... | collective-permute-start | bytes 249608 | tf_op jit(solution)/shard_map/ppermute | solution.py:45
  40.8 7.2 %collective-permute-start.4 = (f32[5,1,18,130]{3,2,1,0:T(8,128)S(1)}, f32[5,1,18,130]{3,2,1,0:T(8,128)S(1)}, u32[]{:S(2)}, u32[]{:S(2)}) collective-permute-start(f32[5,1,18,130]{3,2,1,0:T(8,128)S(1)} %get-tuple-element.72), channel_id=1, source_target_pairs={{1,0},{2,1},{3,2},{5,4},{6,5},{7,6},{9,8},{10,9},{11,10},{13,12},{... | collective-permute-start | bytes 140408 | tf_op jit(solution)/shard_map/ppermute | solution.py:48
  42.1 7.0 %collective-permute-start.5 = (f32[5,1,18,130]{3,2,1,0:T(8,128)S(1)}, f32[5,1,18,130]{3,2,1,0:T(8,128)S(1)}, u32[]{:S(2)}, u32[]{:S(2)}) collective-permute-start(f32[5,1,18,130]{3,2,1,0:T(8,128)S(1)} %get-tuple-element.71), channel_id=1, source_target_pairs={{0,1},{1,2},{2,3},{4,5},{5,6},{6,7},{8,9},{9,10},{10,11},{12,13},{... | collective-permute-start | bytes 140408 | tf_op jit(solution)/shard_map/ppermute | solution.py:45
  100.3 7.7 %collective-permute-start.6 = (f32[5,32,16,1]{1,2,3,0:T(8,128)S(1)}, f32[5,32,16,1]{1,2,3,0:T(8,128)S(1)}, u32[]{:S(2)}, u32[]{:S(2)}) collective-permute-start(f32[5,32,16,1]{1,2,3,0:T(8,128)S(1)} %copy.44), channel_id=1, source_target_pairs={{64,0},{128,64},{192,128},{256,192},{320,256},{384,320},{448,384},... | collective-permute-start | bytes 30728 | tf_op jit(solution)/shard_map/ppermute | solution.py:48
  103.4 6.2 %collective-permute-start.7 = (f32[5,32,16,1]{1,2,3,0:T(8,128)S(1)}, f32[5,32,16,1]{1,2,3,0:T(8,128)S(1)}, u32[]{:S(2)}, u32[]{:S(2)}) collective-permute-start(f32[5,32,16,1]{1,2,3,0:T(8,128)S(1)} %copy.46), channel_id=1, source_target_pairs={{0,64},{64,128},{128,192},{192,256},{256,320},{320,384},{384,448},... | collective-permute-start | bytes 30728 | tf_op jit(solution)/shard_map/ppermute | solution.py:45
  114.2 4.9 %collective-permute-start.8 = (f32[5,32,1,130]{3,2,1,0:T(1,128)S(1)}, f32[5,32,1,130]{3,2,1,0:T(1,128)S(1)}, u32[]{:S(2)}, u32[]{:S(2)}) collective-permute-start(f32[5,32,1,130]{3,2,1,0:T(1,128)S(1)} %get-tuple-element.76), channel_id=1, source_target_pairs={{4,0},{8,4},{12,8},{16,12},{20,16},{24,20},{28,24},{32,28},{36,32}... | collective-permute-start | bytes 249608 | tf_op jit(solution)/shard_map/ppermute | solution.py:48
  116.2 7.8 %collective-permute-start.9 = (f32[5,32,1,130]{3,2,1,0:T(1,128)S(1)}, f32[5,32,1,130]{3,2,1,0:T(1,128)S(1)}, u32[]{:S(2)}, u32[]{:S(2)}) collective-permute-start(f32[5,32,1,130]{3,2,1,0:T(1,128)S(1)} %get-tuple-element.75), channel_id=1, source_target_pairs={{0,4},{4,8},{8,12},{12,16},{16,20},{20,24},{24,28},{28,32},{32,36}... | collective-permute-start | bytes 249608 | tf_op jit(solution)/shard_map/ppermute | solution.py:45
  124.2 7.4 %collective-permute-start.10 = (f32[5,1,18,130]{3,2,1,0:T(8,128)S(1)}, f32[5,1,18,130]{3,2,1,0:T(8,128)S(1)}, u32[]{:S(2)}, u32[]{:S(2)}) collective-permute-start(f32[5,1,18,130]{3,2,1,0:T(8,128)S(1)} %get-tuple-element.70), channel_id=1, source_target_pairs={{1,0},{2,1},{3,2},{5,4},{6,5},{7,6},{9,8},{10,9},{11,10},{13,12},{... | collective-permute-start | bytes 140408 | tf_op jit(solution)/shard_map/ppermute | solution.py:48
  125.5 7.4 %collective-permute-start.11 = (f32[5,1,18,130]{3,2,1,0:T(8,128)S(1)}, f32[5,1,18,130]{3,2,1,0:T(8,128)S(1)}, u32[]{:S(2)}, u32[]{:S(2)}) collective-permute-start(f32[5,1,18,130]{3,2,1,0:T(8,128)S(1)} %get-tuple-element.69), channel_id=1, source_target_pairs={{0,1},{1,2},{2,3},{4,5},{5,6},{6,7},{8,9},{9,10},{10,11},{12,13},{... | collective-permute-start | bytes 140408 | tf_op jit(solution)/shard_map/ppermute | solution.py:45
  154.3 4.3 %collective-permute-start.12 = (f32[1,1,1,2048]{3,2,1,0:T(1,128)S(1)}, f32[1,1,1,2048]{3,2,1,0:T(1,128)S(1)}, u32[]{:S(2)}, u32[]{:S(2)}) collective-permute-start(f32[1,1,1,2048]{3,2,1,0:T(1,128)S(1)} %bitcast.173), channel_id=1, source_target_pairs={{0,4},{4,8},{8,12},{12,16},{16,20},{20,24},{24,28},{28,32},{32,36}... | collective-permute-start | bytes 24584 | tf_op jit(solution)/shard_map/ppermute | solution.py:28
  154.3 4.3 %collective-permute-start.13 = (f32[1,1,1,2048]{3,2,1,0:T(1,128)S(1)}, f32[1,1,1,2048]{3,2,1,0:T(1,128)S(1)}, u32[]{:S(2)}, u32[]{:S(2)}) collective-permute-start(f32[1,1,1,2048]{3,2,1,0:T(1,128)S(1)} %bitcast.174), channel_id=1, source_target_pairs={{0,60},{4,0},{8,4},{12,8},{16,12},{20,16},{24,20},{28,24},{32,28},... | collective-permute-start | bytes 24584 | tf_op jit(solution)/shard_map/ppermute | solution.py:33
  158.6 4.3 %collective-permute-start.14 = (f32[1,1,1,2048]{3,2,1,0:T(1,128)S(1)}, f32[1,1,1,2048]{3,2,1,0:T(1,128)S(1)}, u32[]{:S(2)}, u32[]{:S(2)}) collective-permute-start(f32[1,1,1,2048]{3,2,1,0:T(1,128)S(1)} %collective-permute-done.12), channel_id=1, source_target_pairs={{0,4},{4,8},{8,12},{12,16},{16,20},{20,24},{24,28},{28,32},{32,36}... | collective-permute-start | bytes 24584 | tf_op jit(solution)/shard_map/ppermute | solution.py:28
  158.6 4.3 %collective-permute-start.15 = (f32[1,1,1,2048]{3,2,1,0:T(1,128)S(1)}, f32[1,1,1,2048]{3,2,1,0:T(1,128)S(1)}, u32[]{:S(2)}, u32[]{:S(2)}) collective-permute-start(f32[1,1,1,2048]{3,2,1,0:T(1,128)S(1)} %collective-permute-done.13), channel_id=1, source_target_pairs={{0,60},{4,0},{8,4},{12,8},{16,12},{20,16},{24,20},{28,24},{32,28},... | collective-permute-start | bytes 24584 | tf_op jit(solution)/shard_map/ppermute | solution.py:33
  162.8 4.3 %collective-permute-start.16 = (f32[1,1,1,2048]{3,2,1,0:T(1,128)S(1)}, f32[1,1,1,2048]{3,2,1,0:T(1,128)S(1)}, u32[]{:S(2)}, u32[]{:S(2)}) collective-permute-start(f32[1,1,1,2048]{3,2,1,0:T(1,128)S(1)} %collective-permute-done.14), channel_id=1, source_target_pairs={{0,4},{4,8},{8,12},{12,16},{16,20},{20,24},{24,28},{28,32},{32,36}... | collective-permute-start | bytes 24584 | tf_op jit(solution)/shard_map/ppermute | solution.py:28
  162.9 4.3 %collective-permute-start.17 = (f32[1,1,1,2048]{3,2,1,0:T(1,128)S(1)}, f32[1,1,1,2048]{3,2,1,0:T(1,128)S(1)}, u32[]{:S(2)}, u32[]{:S(2)}) collective-permute-start(f32[1,1,1,2048]{3,2,1,0:T(1,128)S(1)} %collective-permute-done.15), channel_id=1, source_target_pairs={{0,60},{4,0},{8,4},{12,8},{16,12},{20,16},{24,20},{28,24},{32,28},... | collective-permute-start | bytes 24584 | tf_op jit(solution)/shard_map/ppermute | solution.py:33
  167.1 4.3 %collective-permute-start.18 = (f32[1,1,1,2048]{3,2,1,0:T(1,128)S(1)}, f32[1,1,1,2048]{3,2,1,0:T(1,128)S(1)}, u32[]{:S(2)}, u32[]{:S(2)}) collective-permute-start(f32[1,1,1,2048]{3,2,1,0:T(1,128)S(1)} %collective-permute-done.16), channel_id=1, source_target_pairs={{0,4},{4,8},{8,12},{12,16},{16,20},{20,24},{24,28},{28,32},{32,36}... | collective-permute-start | bytes 24584 | tf_op jit(solution)/shard_map/ppermute | solution.py:28
  167.2 4.3 %collective-permute-start.19 = (f32[1,1,1,2048]{3,2,1,0:T(1,128)S(1)}, f32[1,1,1,2048]{3,2,1,0:T(1,128)S(1)}, u32[]{:S(2)}, u32[]{:S(2)}) collective-permute-start(f32[1,1,1,2048]{3,2,1,0:T(1,128)S(1)} %collective-permute-done.17), channel_id=1, source_target_pairs={{0,60},{4,0},{8,4},{12,8},{16,12},{20,16},{24,20},{28,24},{32,28},... | collective-permute-start | bytes 24584 | tf_op jit(solution)/shard_map/ppermute | solution.py:33
  171.4 4.3 %collective-permute-start.20 = (f32[1,1,1,2048]{3,2,1,0:T(1,128)S(1)}, f32[1,1,1,2048]{3,2,1,0:T(1,128)S(1)}, u32[]{:S(2)}, u32[]{:S(2)}) collective-permute-start(f32[1,1,1,2048]{3,2,1,0:T(1,128)S(1)} %collective-permute-done.18), channel_id=1, source_target_pairs={{0,4},{4,8},{8,12},{12,16},{16,20},{20,24},{24,28},{28,32},{32,36}... | collective-permute-start | bytes 24584 | tf_op jit(solution)/shard_map/ppermute | solution.py:28
  175.7 4.3 %collective-permute-start.22 = (f32[1,1,1,2048]{3,2,1,0:T(1,128)S(1)}, f32[1,1,1,2048]{3,2,1,0:T(1,128)S(1)}, u32[]{:S(2)}, u32[]{:S(2)}) collective-permute-start(f32[1,1,1,2048]{3,2,1,0:T(1,128)S(1)} %collective-permute-done.20), channel_id=1, source_target_pairs={{0,4},{4,8},{8,12},{12,16},{16,20},{20,24},{24,28},{28,32},{32,36}... | collective-permute-start | bytes 24584 | tf_op jit(solution)/shard_map/ppermute | solution.py:28
  180.0 7.4 %collective-permute-start.25 = (f32[1,1,1,2048]{3,2,1,0:T(1,128)S(1)}, f32[1,1,1,2048]{3,2,1,0:T(1,128)S(1)}, u32[]{:S(2)}, u32[]{:S(2)}) collective-permute-start(f32[1,1,1,2048]{3,2,1,0:T(1,128)S(1)} %collective-permute-done.23), channel_id=1, source_target_pairs={{0,60},{4,0},{8,4},{12,8},{16,12},{20,16},{24,20},{28,24},{32,28},... | collective-permute-start | bytes 24584 | tf_op jit(solution)/shard_map/ppermute | solution.py:33
  (22 other events, 467.6 us)
